TPU v7x, 256 devices: a whole 4x4x8 slice. The times are simulated.
256 devices in a mesh: ctx: 16 (over z, core), exp: 16 (over x, y).
Axes of the slice: x: 4, y: 4, z: 8, core: 2. Of those that a mesh axis runs over, the one named last changes fastest.
Arguments:
- query_input: bfloat16 [2048, 8192], P('ctx', 'exp'), may hold values from -6 to 6
- key_input: bfloat16 [2048, 8192], P('ctx', 'exp'), may hold values from -6 to 6
- value_input: bfloat16 [2048, 8192], P('ctx', 'exp'), may hold values from -6 to 6
- gate_logits: float32 [2, 2048, 64], P(None, 'ctx', 'exp'), may hold values from -6 to 6
- comp_weight: float32 [2, 32, 64], P(None, None, 'exp'), may hold values from -6 to 6
- out_proj: bfloat16 [8192, 7168], P('exp', 'ctx'), may hold values from -0.0625 to 0.0625
- residual_in: bfloat16 [2048, 7168], P(('ctx', 'exp')), may hold values from -3 to 3
- ffn_gain: float32 [7168], replicated, may hold values from 0.25 to 1.75
- expert_ids: int32 [2048, 2], P(('ctx', 'exp')), may hold values from 0 to 15, all different within a row; in each aligned block of 8 rows (0 to 7, 8 to 15, ...) at most 2 rows name the same one
- route_gates: float32 [2048, 2], P(('ctx', 'exp')), may hold values from 0.2 to 1
- expert_gate: bfloat16 [16, 7168, 2048], P('exp', None, 'ctx'), may hold values from -0.0625 to 0.0625
- expert_up: bfloat16 [16, 7168, 2048], P('exp', None, 'ctx'), may hold values from -0.0625 to 0.0625
- expert_down: bfloat16 [16, 2048, 7168], P('exp', 'ctx'), may hold values from -0.125 to 0.125
Outputs:
- layer_out: bfloat16 [2048, 7168], P(('ctx', 'exp'))
Inputs may be any that keep to these rules, and one draw needn't show every extreme that they name: `expert_ids`: each token names 2 different experts. In every aligned block of 8 consecutive tokens no expert is named more than 2 times, a bound that some block reaches.
All inputs are finite; a program needn't handle non-finite values.
Results may differ from a plain program's by a relative error of at most 0.0085.
Values may be sent and summed in bfloat16 or wider, within the bound.
A program may use at most 128 MiB of HBM per device.

v0:
```python
import math
import jax
import jax.numpy as jnp
from jax import lax
from jax.sharding import PartitionSpec as P

WINDOW = 512
score_gain = 2.0
norm_eps = 1e-06


def passed_along(block, axis, distance):
    devices = range(lax.axis_size(axis))
    route = [(i - distance, i) for i in devices if i - distance in devices]
    return lax.ppermute(block, axis, route)


def head_norm(matrix, head_width):
    row_count = matrix.shape[0]
    shaped = matrix.reshape(row_count, -1, head_width).astype(jnp.float32)
    scaled = shaped * lax.rsqrt(jnp.mean(shaped * shaped, axis=2, keepdims=True) + norm_eps)
    return scaled.reshape(row_count, -1)


def compress(extended, position_weights, head_width):
    stride_len = position_weights.shape[0] // 2
    head_count = position_weights.shape[1]
    blocks = extended.reshape(-1, stride_len, head_count, head_width).astype(jnp.float32)
    first_half = jnp.einsum(
        "nshd,sh->nhd", blocks[:-1], position_weights[:stride_len], precision=lax.Precision.HIGHEST
    )
    second_half = jnp.einsum(
        "nshd,sh->nhd", blocks[1:], position_weights[stride_len:], precision=lax.Precision.HIGHEST
    )
    return (first_half + second_half).reshape(blocks.shape[0] - 1, head_count * head_width)


def local(
    query_input,
    key_input,
    value_input,
    gate_logits,
    comp_weight,
    out_proj,
    residual_in,
    ffn_gain,
    expert_ids,
    route_gates,
    expert_gate,
    expert_up,
    expert_down,
):
    row_count = query_input.shape[0]
    head_count = comp_weight.shape[2]
    head_width = query_input.shape[1] // head_count
    block_len = comp_weight.shape[1]
    stride_len = block_len // 2
    exp_count = lax.axis_size("exp")
    ctx_index = lax.axis_index("ctx")
    scale = score_gain / math.sqrt(head_width)
    query_norm = head_norm(query_input, head_width).astype(jnp.bfloat16)
    key_norm = head_norm(key_input, head_width).astype(jnp.bfloat16)
    next_keys, next_values = passed_along(
        (key_input[:stride_len], value_input[:stride_len]), "ctx", -1
    )
    comp_keys = head_norm(
        compress(jnp.concatenate([key_input, next_keys], 0), comp_weight[0], head_width), head_width
    ).astype(jnp.bfloat16)
    comp_values = compress(
        jnp.concatenate([value_input, next_values], 0), comp_weight[1], head_width
    ).astype(jnp.bfloat16)
    query_pos = ctx_index * row_count + jnp.arange(row_count, dtype=jnp.int32)
    query_heads = query_norm.reshape(row_count, head_count, head_width)
    part_keys = lax.all_gather(comp_keys, "ctx", axis=0, tiled=True)
    part_values = lax.all_gather(comp_values, "ctx", axis=0, tiled=True)
    part_count = part_keys.shape[0]
    scores = jnp.einsum(
        "thd,nhd->htn",
        query_heads,
        part_keys.reshape(part_count, head_count, head_width),
        preferred_element_type=jnp.float32,
    )
    block_end = jnp.arange(part_count, dtype=jnp.int32) * stride_len + block_len - 1
    visible = block_end[None, :] <= query_pos[:, None]
    weights = jnp.where(visible[None], jnp.exp(scale * scores), 0.0)
    running_total = jnp.sum(weights, axis=2).T
    collected = jnp.einsum(
        "htn,nhd->thd",
        weights.astype(jnp.bfloat16),
        part_values.reshape(part_count, head_count, head_width),
        preferred_element_type=jnp.float32,
    )
    cmp_sum = collected.reshape(row_count, -1)
    no_block = (query_pos < block_len - 1).astype(jnp.float32)
    cmp_out = (
        cmp_sum.reshape(row_count, head_count, head_width)
        / (running_total + no_block[:, None])[:, :, None]
    )
    shift_count = max(1, WINDOW // row_count)
    earlier_keys = []
    earlier_values = []
    for distance in range(shift_count, 0, -1):
        moved_keys, moved_values = passed_along((key_norm, value_input), "ctx", distance)
        earlier_keys.append(moved_keys)
        earlier_values.append(moved_values)
    near_keys = jnp.concatenate(earlier_keys + [key_norm], 0)
    near_values = jnp.concatenate(earlier_values + [value_input], 0)
    key_pos = ctx_index * row_count - WINDOW + jnp.arange(near_keys.shape[0], dtype=jnp.int32)
    near_scores = jnp.einsum(
        "thd,shd->hts",
        query_heads,
        near_keys.reshape(-1, head_count, head_width),
        preferred_element_type=jnp.float32,
    )
    inside = (
        (key_pos[None, :] <= query_pos[:, None])
        & (key_pos[None, :] > query_pos[:, None] - WINDOW)
        & (key_pos[None, :] >= 0)
    )
    near_weights = jnp.where(inside[None], jnp.exp(scale * near_scores), 0.0)
    win_total = jnp.sum(near_weights, axis=2).T
    win_sum = jnp.einsum(
        "hts,shd->thd",
        near_weights.astype(jnp.bfloat16),
        near_values.reshape(-1, head_count, head_width),
        preferred_element_type=jnp.float32,
    )
    win_out = win_sum / win_total[:, :, None]
    branch_gates = jax.nn.sigmoid(gate_logits)
    attended = (
        (branch_gates[0][:, :, None] * cmp_out + branch_gates[1][:, :, None] * win_out)
        .reshape(row_count, -1)
        .astype(jnp.bfloat16)
    )
    token_share = row_count // exp_count
    partial_sum = jnp.dot(
        attended,
        lax.all_gather(out_proj, "ctx", axis=1, tiled=True),
        preferred_element_type=jnp.float32,
    )
    projected = lax.psum_scatter(partial_sum, "exp", scatter_dimension=0, tiled=True)
    hidden_state = residual_in.astype(jnp.float32) + projected
    mean_square = jnp.mean(hidden_state * hidden_state, axis=1, keepdims=True)
    normed = (hidden_state * lax.rsqrt(mean_square + norm_eps) * ffn_gain).astype(jnp.bfloat16)
    model_width = normed.shape[1]
    top_count = expert_ids.shape[1]
    capacity = max(2, 2 * token_share * top_count // exp_count)
    flat_ids = expert_ids.reshape(-1)
    chosen = (flat_ids[:, None] == jnp.arange(exp_count, dtype=jnp.int32)[None, :]).astype(
        jnp.int32
    )
    slots = jnp.sum((jnp.cumsum(chosen, axis=0) - chosen) * chosen, axis=1)
    targets = (flat_ids * capacity + slots).reshape(token_share, top_count)
    slot_range = jnp.arange(exp_count * capacity, dtype=jnp.int32)
    dispatch_map = jnp.sum(
        (slot_range[:, None, None] == targets[None, :, :]).astype(jnp.float32), axis=2
    ).astype(jnp.bfloat16)
    outgoing = (
        jnp.dot(dispatch_map, normed, preferred_element_type=jnp.float32)
        .astype(jnp.bfloat16)
        .reshape(exp_count, capacity, model_width)
    )
    arrived = lax.all_to_all(outgoing, "exp", split_axis=0, concat_axis=0, tiled=True)
    gate_cols = expert_gate[0]
    up_cols = expert_up[0]
    down_rows = expert_down[0]
    portion = lax.all_gather(arrived, "ctx", axis=0, tiled=True)
    flat_rows = portion.reshape(-1, model_width)
    gate_part = jnp.dot(flat_rows, gate_cols, preferred_element_type=jnp.float32)
    up_part = jnp.dot(flat_rows, up_cols, preferred_element_type=jnp.float32)
    activated = (jax.nn.silu(gate_part) * up_part).astype(jnp.bfloat16)
    partial_out = jnp.dot(activated, down_rows, preferred_element_type=jnp.float32).reshape(
        portion.shape
    )
    finished = lax.psum_scatter(
        partial_out.astype(jnp.bfloat16), "ctx", scatter_dimension=0, tiled=True
    )
    returned = lax.all_to_all(finished, "exp", split_axis=0, concat_axis=0, tiled=True).reshape(
        -1, model_width
    )
    combine_map = jnp.sum(
        jnp.where(slot_range[None, None, :] == targets[:, :, None], route_gates[:, :, None], 0.0),
        axis=1,
    )
    moe_out = jnp.dot(combine_map, returned.astype(jnp.float32), precision=lax.Precision.HIGHEST)
    return (hidden_state + moe_out).astype(jnp.bfloat16)


def solution(mesh):
    in_specs = (
        P("ctx", "exp"),
        P("ctx", "exp"),
        P("ctx", "exp"),
        P(None, "ctx", "exp"),
        P(None, None, "exp"),
        P("exp", "ctx"),
        P(("ctx", "exp"), None),
        P(),
        P(("ctx", "exp"), None),
        P(("ctx", "exp"), None),
        P("exp", None, "ctx"),
        P("exp", None, "ctx"),
        P("exp", "ctx", None),
    )
    out_specs = P(("ctx", "exp"), None)
    return jax.shard_map(local, mesh=mesh, in_specs=in_specs, out_specs=out_specs, check_vma=False)
```

profile of v0, /device:TPU:8, one launch (start us, length us, event | category | flops | bytes accessed | tf_op | source)
XLA Modules:
  0.0 412.8 jit_solution(15140837322775450915)
XLA Ops:
  8.4 5.2 %collective-permute-start.6 = (bf16[128,512]{0,1:T(8,128)(2,1)S(1)}, bf16[128,512]{0,1:T(8,128)(2,1)S(1)}, u32[]{:S(2)}, u32[]{:S(2)}) collective-permute-start(bf16[128,512]{0,1:T(8,128)(2,1)S(1)} %fusion.24), channel_id=1, source_target_pairs={{0,64},{16,80},{32,96},{48,112},{64,128},{80,144},{96,160},{112,17... | collective-permute-start | bytes 393224 | tf_op jit(solution)/shard_map/ppermute | solution.py:15
  13.6 3.0 collective-permute-start.7
  16.6 5.0 %collective-permute-start.8 = (bf16[128,512]{0,1:T(8,128)(2,1)S(1)}, bf16[128,512]{0,1:T(8,128)(2,1)S(1)}, u32[]{:S(2)}, u32[]{:S(2)}) collective-permute-start(bf16[128,512]{0,1:T(8,128)(2,1)S(1)} %fusion.24), channel_id=1, source_target_pairs={{0,32},{16,48},{32,64},{48,80},{64,96},{80,112},{96,128},{112,144}... | collective-permute-start | bytes 393224 | tf_op jit(solution)/shard_map/ppermute | solution.py:15
  21.7 3.4 collective-permute-start.2
  38.0 3.6 collective-permute-start.3
  42.1 18.2 %all_gather.13 = bf16[128,512]{1,0:T(8,128)(2,1)S(1)} all-gather(bf16[8,512]{1,0:T(8,128)(2,1)S(1)} %fusion.45), channel_id=1, replica_groups=mesh['ctx'=16,'exp'=16] {'ctx'}, dimensions={0}, use_global_device_ids=true | all-gather | bytes 139264 | tf_op jit(solution)/shard_map/all_gather | solution.py:74
  61.3 2.9 collective-permute-start.4
  64.2 2.0 collective-permute-start.5
  66.2 4.5 %collective-permute-done.4 = bf16[128,512]{1,0:T(8,128)(2,1)S(1)} collective-permute-done((bf16[128,512]{1,0:T(8,128)(2,1)S(1)}, bf16[128,512]{1,0:T(8,128)(2,1)S(1)}, u32[]{:S(2)}, u32[]{:S(2)}) %collective-permute-start.4) | collective-permute-done | bytes 131104 | tf_op jit(solution)/shard_map/ppermute | solution.py:15
  70.8 1.9 collective-permute-start.9
  74.1 4.0 collective-permute-done
  79.8 19.0 %all_gather.12 = bf16[128,512]{1,0:T(8,128)(2,1)S(1)} all-gather(bf16[8,512]{1,0:T(8,128)(2,1)S(1)} %fusion.44), channel_id=1, replica_groups=mesh['ctx'=16,'exp'=16] {'ctx'}, dimensions={0}, use_global_device_ids=true | all-gather | bytes 139264 | tf_op jit(solution)/shard_map/all_gather | solution.py:75
  104.6 7.5 %fusion.52 = f32[128,7168]{1,0:T(8,128)} fusion(bf16[128,512]{0,1:T(8,128)(2,1)S(1)} %bitcast.126, bf16[512,7168]{0,1:T(8,128)(2,1)} %all-gather.3.cloned.1.call-done), kind=kOutput, calls=%fused_computation.101 | convolution fusion | flops 939524096 | bytes 11141120 | tf_op jit(solution)/shard_map/dot_general | solution.py:136
  114.8 107.4 %all-reduce.3.cloned.1.call-done = f32[128,7168]{1,0:T(8,128)} async-done(((f32[128,7168]{1,0:T(8,128)}), f32[128,7168]{1,0:T(8,128)}) %all-reduce.3.cloned.1.call-update) | async-done | bytes 3670032
  224.7 15.1 %all_to_all.10 = bf16[16,2,7168]{2,1,0:T(2,128)(2,1)} all-to-all(bf16[16,2,7168]{2,1,0:T(2,128)(2,1)S(1)} %reshape.231), channel_id=1, replica_groups=mesh['ctx'=16,'exp'=16] {'exp'}, dimensions={0} | all-to-all | bytes 917504 | tf_op jit(solution)/shard_map/all_to_all | solution.py:163
  240.1 49.7 %all-gather.5.cloned.1.call-done = bf16[256,2,7168]{2,1,0:T(2,128)(2,1)} async-done(((bf16[16,2,7168]{2,1,0:T(2,128)(2,1)}), bf16[256,2,7168]{2,1,0:T(2,128)(2,1)}) %all-gather.5.cloned.1.call-update) | async-done | bytes 7340048 | tf_op jit(solution)/shard_map/all_gather | solution.py:167
  289.8 15.4 %reshape.232 = bf16[512,7168]{1,0:T(8,128)(2,1)} reshape(bf16[256,2,7168]{2,1,0:T(2,128)(2,1)} %all-gather.5.cloned.1.call-done) | data formatting | bytes 14680064 | tf_op jit(solution)/shard_map/reshape | solution.py:168
  305.2 5.8 %fusion.4 = f32[512,128]{1,0:T(8,128)S(1)} fusion(bf16[512,7168]{1,0:T(8,128)(2,1)} %reshape.232, bf16[1,7168,128]{2,1,0:T(8,128)(2,1)} %param.23), kind=kOutput, calls=%fused_computation.7 | convolution fusion | flops 939524096 | bytes 9437184 | tf_op jit(solution)/shard_map/dot_general | solution.py:169
  311.4 2.1 fusion.19
  313.4 5.0 %convolution_convert_fusion = bf16[256,2,7168]{2,0,1:T(8,128)(2,1)} fusion(bf16[1,128,7168]{2,1,0:T(8,128)(2,1)S(1)} %copy-done, bf16[256,2,128]{2,1,0:T(2,128)(2,1)S(1)} %bitcast.127), kind=kOutput, calls=%fused_computation | convolution fusion | flops 943194112 | bytes 9306112 | tf_op jit(solution)/shard_map/dot_general | solution.py:172
  318.5 67.8 %reduce-scatter.2.cloned.1.call-done = bf16[16,2,7168]{2,0,1:T(8,128)(2,1)} async-done(((bf16[256,2,7168]{2,0,1:T(8,128)(2,1)}), bf16[16,2,7168]{2,0,1:T(8,128)(2,1)}) %reduce-scatter.2.cloned.1.call-update) | async-done | bytes 458768 | tf_op jit(solution)/shard_map/reduce_scatter | solution.py:175
  386.3 2.3 copy.99
  388.6 7.3 %all-to-all-start.1 = ((bf16[16,2,7168]{2,1,0:T(2,128)(2,1)}), bf16[16,2,7168]{2,1,0:T(2,128)(2,1)S(1)}, u32[]{:S(2)}, u32[]{:S(2)}) async-start(bf16[16,2,7168]{2,1,0:T(2,128)(2,1)} %copy.99), calls=%async_computation.2 | async-start | bytes 917504 | tf_op jit(solution)/shard_map/all_to_all | solution.py:178
  395.9 8.3 %all-to-all-done.1 = bf16[16,2,7168]{2,1,0:T(2,128)(2,1)S(1)} async-done(((bf16[16,2,7168]{2,1,0:T(2,128)(2,1)}), bf16[16,2,7168]{2,1,0:T(2,128)(2,1)S(1)}, u32[]{:S(2)}, u32[]{:S(2)}) %all-to-all-start.1) | async-done | bytes 458784 | tf_op jit(solution)/shard_map/all_to_all | solution.py:178
  (122 shorter events, 32.1 us)
Async XLA Ops:
  6.5 306.9 %copy-start = (bf16[1,128,7168]{2,1,0:T(8,128)(2,1)S(1)}, bf16[1,128,7168]{2,1,0:T(8,128)(2,1)}, u32[]{:S(2)}) copy-start(bf16[1,128,7168]{2,1,0:T(8,128)(2,1)} %param.25) | copy-start | bytes 5505028
  6.5 35.1 %copy-start.2 = (bf16[128,512]{1,0:T(8,128)(2,1)S(1)}, bf16[128,512]{1,0:T(8,128)(2,1)}, u32[]{:S(2)}) copy-start(bf16[128,512]{1,0:T(8,128)(2,1)} %param.14) | copy-start | bytes 393220
  6.5 30.8 %copy-start.4 = (bf16[128,512]{1,0:T(8,128)(2,1)S(1)}, bf16[128,512]{1,0:T(8,128)(2,1)}, u32[]{:S(2)}) copy-start(bf16[128,512]{1,0:T(8,128)(2,1)} %param.15) | copy-start | bytes 393220
  6.5 30.7 %copy-start.5 = (bf16[128,512]{1,0:T(8,128)(2,1)S(1)}, bf16[128,512]{1,0:T(8,128)(2,1)}, u32[]{:S(2)}) copy-start(bf16[128,512]{1,0:T(8,128)(2,1)} %param.13) | copy-start | bytes 393220
  6.5 98.1 %all-gather.3.cloned.1.call-start = ((), (), s32[]{:S(2)}) async-start(), calls=%async_computation.3 | async-start | bytes 7798784 | tf_op jit(solution)/shard_map/all_gather | solution.py:138
  7.3 214.9 %all-reduce.3.cloned.1.call-start = ((), (), s32[]{:S(2)}) async-start(), calls=%async_computation.6 | async-start | bytes 7340032
  8.4 71.3 %collective-permute-start.6 = (bf16[128,512]{0,1:T(8,128)(2,1)S(1)}, bf16[128,512]{0,1:T(8,128)(2,1)S(1)}, u32[]{:S(2)}, u32[]{:S(2)}) collective-permute-start(bf16[128,512]{0,1:T(8,128)(2,1)S(1)} %fusion.24), channel_id=1, source_target_pairs={{0,64},{16,80},{32,96},{48,112},{64,128},{80,144},{96,160},{112,17... | collective-permute-start | bytes 393224 | tf_op jit(solution)/shard_map/ppermute | solution.py:15
  13.6 66.2 %collective-permute-start.7 = (bf16[128,512]{0,1:T(8,128)(2,1)S(1)}, bf16[128,512]{0,1:T(8,128)(2,1)S(1)}, u32[]{:S(2)}, u32[]{:S(2)}) collective-permute-start(bf16[128,512]{0,1:T(8,128)(2,1)S(1)} %fusion.24), channel_id=1, source_target_pairs={{0,48},{16,64},{32,80},{48,96},{64,112},{80,128},{96,144},{112,160... | collective-permute-start | bytes 393224 | tf_op jit(solution)/shard_map/ppermute | solution.py:15
  16.6 82.7 %collective-permute-start.8 = (bf16[128,512]{0,1:T(8,128)(2,1)S(1)}, bf16[128,512]{0,1:T(8,128)(2,1)S(1)}, u32[]{:S(2)}, u32[]{:S(2)}) collective-permute-start(bf16[128,512]{0,1:T(8,128)(2,1)S(1)} %fusion.24), channel_id=1, source_target_pairs={{0,32},{16,48},{32,64},{48,80},{64,96},{80,112},{96,128},{112,144}... | collective-permute-start | bytes 393224 | tf_op jit(solution)/shard_map/ppermute | solution.py:15
  21.7 39.6 %collective-permute-start.2 = (bf16[128,512]{1,0:T(8,128)(2,1)}, bf16[128,512]{1,0:T(8,128)(2,1)S(1)}, u32[]{:S(2)}, u32[]{:S(2)}) collective-permute-start(bf16[128,512]{1,0:T(8,128)(2,1)} %param.15), channel_id=1, source_target_pairs={{0,64},{16,80},{32,96},{48,112},{64,128},{80,144},{96,160},{112,17... | collective-permute-start | bytes 393224 | tf_op jit(solution)/shard_map/ppermute | solution.py:15
  26.4 11.6 %collective-permute-start.1 = (bf16[16,512]{1,0:T(8,128)(2,1)}, bf16[16,512]{1,0:T(8,128)(2,1)S(1)}, u32[]{:S(2)}, u32[]{:S(2)}) collective-permute-start(bf16[16,512]{1,0:T(8,128)(2,1)} %slice.74), channel_id=1, source_target_pairs={{16,0},{32,16},{48,32},{64,48},{80,64},{96,80},{112,96},{128,112},... | collective-permute-start | bytes 49160 | tf_op jit(solution)/shard_map/ppermute | solution.py:15
  38.0 26.2 %collective-permute-start.3 = (bf16[128,512]{1,0:T(8,128)(2,1)S(1)}, bf16[128,512]{1,0:T(8,128)(2,1)S(1)}, u32[]{:S(2)}, u32[]{:S(2)}) collective-permute-start(bf16[128,512]{1,0:T(8,128)(2,1)S(1)} %copy-done.4), channel_id=1, source_target_pairs={{0,48},{16,64},{32,80},{48,96},{64,112},{80,128},{96,144},{112,160... | collective-permute-start | bytes 393224 | tf_op jit(solution)/shard_map/ppermute | solution.py:15
  61.3 42.7 %copy-start.10 = (f32[128,4]{0,1:T(4,128)S(1)}, f32[128,4]{0,1:T(4,128)}, u32[]{:S(2)}) copy-start(f32[128,4]{0,1:T(4,128)} %get-tuple-element.8) | copy-start | bytes 6148
  61.3 9.5 %collective-permute-start.4 = (bf16[128,512]{1,0:T(8,128)(2,1)S(1)}, bf16[128,512]{1,0:T(8,128)(2,1)S(1)}, u32[]{:S(2)}, u32[]{:S(2)}) collective-permute-start(bf16[128,512]{1,0:T(8,128)(2,1)S(1)} %copy-done.4), channel_id=1, source_target_pairs={{0,32},{16,48},{32,64},{48,80},{64,96},{80,112},{96,128},{112,144}... | collective-permute-start | bytes 393224 | tf_op jit(solution)/shard_map/ppermute | solution.py:15
  64.2 8.5 %collective-permute-start.5 = (bf16[128,512]{1,0:T(8,128)(2,1)S(1)}, bf16[128,512]{1,0:T(8,128)(2,1)S(1)}, u32[]{:S(2)}, u32[]{:S(2)}) collective-permute-start(bf16[128,512]{1,0:T(8,128)(2,1)S(1)} %copy-done.4), channel_id=1, source_target_pairs={{0,16},{16,32},{32,48},{48,64},{64,80},{80,96},{96,112},{112,128},... | collective-permute-start | bytes 393224 | tf_op jit(solution)/shard_map/ppermute | solution.py:15
  70.8 29.3 %collective-permute-start.9 = (bf16[128,512]{0,1:T(8,128)(2,1)S(1)}, bf16[128,512]{0,1:T(8,128)(2,1)}, u32[]{:S(2)}, u32[]{:S(2)}) collective-permute-start(bf16[128,512]{0,1:T(8,128)(2,1)S(1)} %fusion.24), channel_id=1, source_target_pairs={{0,16},{16,32},{32,48},{48,64},{64,80},{80,96},{96,112},{112,128},... | collective-permute-start | bytes 393224 | tf_op jit(solution)/shard_map/ppermute | solution.py:15
  72.7 5.4 %collective-permute-start = (bf16[16,512]{1,0:T(8,128)(2,1)}, bf16[16,512]{1,0:T(8,128)(2,1)S(1)}, u32[]{:S(2)}, u32[]{:S(2)}) collective-permute-start(bf16[16,512]{1,0:T(8,128)(2,1)} %slice.66), channel_id=1, source_target_pairs={{16,0},{32,16},{48,32},{64,48},{80,64},{96,80},{112,96},{128,112},... | collective-permute-start | bytes 49160 | tf_op jit(solution)/shard_map/ppermute | solution.py:15
  79.8 24.6 %copy-start.9 = (f32[128,4]{0,1:T(4,128)S(1)}, f32[128,4]{0,1:T(4,128)}, u32[]{:S(2)}) copy-start(f32[128,4]{0,1:T(4,128)} %get-tuple-element.7) | copy-start | bytes 6148
  112.1 110.0 %copy-start.3 = (bf16[8,7168]{1,0:T(8,128)(2,1)S(1)}, bf16[8,7168]{1,0:T(8,128)(2,1)}, u32[]{:S(2)}) copy-start(bf16[8,7168]{1,0:T(8,128)(2,1)} %param.19) | copy-start | bytes 344068
  112.1 111.1 %copy-start.7 = (f32[7168]{0:T(1024)S(1)}, f32[7168]{0:T(1024)}, u32[]{:S(2)}) copy-start(f32[7168]{0:T(1024)} %param.20) | copy-start | bytes 86020
  112.2 177.6 %all-gather.5.cloned.1.call-start = ((), (), s32[]{:S(2)}) async-start(), calls=%async_computation.4 | async-start | bytes 7798784 | tf_op jit(solution)/shard_map/all_gather | solution.py:167
  239.8 146.4 %reduce-scatter.2.cloned.1.call-start = ((), (), s32[]{:S(2)}) async-start(), calls=%async_computation.5 | async-start | bytes 7798784 | tf_op jit(solution)/shard_map/reduce_scatter | solution.py:175
  318.4 77.4 %copy-start.12 = (f32[8,2]{0,1:T(2,128)S(1)}, f32[8,2]{0,1:T(2,128)}, u32[]{:S(2)}) copy-start(f32[8,2]{0,1:T(2,128)} %param.22) | copy-start | bytes 196
  388.6 15.6 %all-to-all-start.1 = ((bf16[16,2,7168]{2,1,0:T(2,128)(2,1)}), bf16[16,2,7168]{2,1,0:T(2,128)(2,1)S(1)}, u32[]{:S(2)}, u32[]{:S(2)}) async-start(bf16[16,2,7168]{2,1,0:T(2,128)(2,1)} %copy.99), calls=%async_computation.2 | async-start | bytes 917504 | tf_op jit(solution)/shard_map/all_to_all | solution.py:178
  (7 other events, 62.2 us)
Sparse Core Ops, SparseCore 0:
  9.2 68.1 all-gather.2
  112.3 109.8 all-reduce.2
  240.0 49.7 all-gather.4
  318.6 67.6 reduce-scatter.1
where the time goes:
time: 414 us; the launch traced here: 413 us
  waiting for transfers between devices  243 us (59%)
  blocking collectives  52.3 us (13%)
  starting transfers between devices  37.2 us (9%)
  local copies, waits for them, and re-layouts  31.5 us (8%)
  matrix products  29.6 us (7%)
  between operations  14.3 us (3%)
  other arithmetic  5.39 us (1%)
    unnamed x5, waiting for transfers between devices  108 us
    reduce_scatter x1, waiting for transfers between devices, local(): lax.psum_scatter(partial_out.astype(jnp.bfloat16), 'ctx', scatter_dimensi...  67.8 us
    all_gather x1, waiting for transfers between devices, local(): portion = lax.all_gather(arrived, 'ctx', axis=0, tiled=True)  49.7 us
    ppermute x10, starting transfers between devices, passed_along(): return lax.ppermute(block, axis, route)  29.6 us
    all_gather x1, blocking collectives, local(): part_values = lax.all_gather(comp_values, 'ctx', axis=0, tiled=True)  19 us
    all_gather x1, blocking collectives, local(): part_keys = lax.all_gather(comp_keys, 'ctx', axis=0, tiled=True)  18.2 us
    reshape x1, local copies, waits for them, and re-layouts, local(): flat_rows = portion.reshape(-1, model_width)  15.4 us
    all_to_all x1, blocking collectives, local(): lax.all_to_all(outgoing, 'exp', split_axis=0, concat_axis=0, tiled=True)  15.1 us
  transfers between devices with their start and end apart: 15, of which 6 were waited for; matrix products, arithmetic and copies ran while one was open for 6% of the time, Pallas kernels for 0%

commit v1 on v0

--- a/solution.py
+++ b/solution.py
@@ -71,8 +71,13 @@
     ).astype(jnp.bfloat16)
     query_pos = ctx_index * row_count + jnp.arange(row_count, dtype=jnp.int32)
     query_heads = query_norm.reshape(row_count, head_count, head_width)
-    part_keys = lax.all_gather(comp_keys, "ctx", axis=0, tiled=True)
-    part_values = lax.all_gather(comp_values, "ctx", axis=0, tiled=True)
+    part_keys, part_values = jnp.split(
+        lax.all_gather(
+            jnp.concatenate([comp_keys, comp_values], axis=1), "ctx", axis=0, tiled=True
+        ),
+        [comp_keys.shape[1]],
+        axis=1,
+    )
     part_count = part_keys.shape[0]
     scores = jnp.einsum(
         "thd,nhd->htn",

time: 414 us -> 400 us (0.966)
  blocking collectives: 52.3 us -> 35.7 us
    all_gather x2 -> x1, blocking collectives: 37.3 us -> 20.7 us  [local(): lax.all_gather(jnp.concatenate([comp_keys, comp_values], axis=1), 'ctx',...]
  transfers between devices with their start and end apart: 15 -> 15, of which waited for: 6 -> 7; matrix products, arithmetic and copies ran while one was open for 6% -> 6% of each run, Pallas kernels for 0% -> 0%
where the time goes in v1:
time: 400 us; the launch traced here: 399 us
  waiting for transfers between devices  243 us (61%)
  starting transfers between devices  38.7 us (10%)
  blocking collectives  35.7 us (9%)
  local copies, waits for them, and re-layouts  31.9 us (8%)
  matrix products  28.4 us (7%)
  between operations  14.3 us (4%)
  other arithmetic  7.15 us (2%)
    unnamed x5, waiting for transfers between devices  108 us
    reduce_scatter x1, waiting for transfers between devices, local(): lax.psum_scatter(partial_out.astype(jnp.bfloat16), 'ctx', scatter_dimensi...  67.8 us
    all_gather x1, waiting for transfers between devices, local(): portion = lax.all_gather(arrived, 'ctx', axis=0, tiled=True)  49.7 us
    ppermute x10, starting transfers between devices, passed_along(): return lax.ppermute(block, axis, route)  31.1 us
    all_gather x1, blocking collectives, local(): lax.all_gather(jnp.concatenate([comp_keys, comp_values], axis=1), 'ctx',...  20.7 us
    reshape x1, local copies, waits for them, and re-layouts, local(): flat_rows = portion.reshape(-1, model_width)  15.4 us
    all_to_all x1, blocking collectives, local(): lax.all_to_all(outgoing, 'exp', split_axis=0, concat_axis=0, tiled=True)  15.1 us
    ppermute x10, waiting for transfers between devices, passed_along(): return lax.ppermute(block, axis, route)  9.42 us
  transfers between devices with their start and end apart: 15, of which 7 were waited for; matrix products, arithmetic and copies ran while one was open for 6% of the time, Pallas kernels for 0%

profile of v1, /device:TPU:8, one launch (start us, length us, event | category | flops | bytes accessed | tf_op | source)
XLA Modules:
  0.0 399.2 jit_solution(6699624199861168681)
XLA Ops:
  8.4 5.2 %collective-permute-start.6 = (bf16[128,512]{0,1:T(8,128)(2,1)S(1)}, bf16[128,512]{0,1:T(8,128)(2,1)S(1)}, u32[]{:S(2)}, u32[]{:S(2)}) collective-permute-start(bf16[128,512]{0,1:T(8,128)(2,1)S(1)} %fusion.24), channel_id=1, source_target_pairs={{0,64},{16,80},{32,96},{48,112},{64,128},{80,144},{96,160},{112,17... | collective-permute-start | bytes 393224 | tf_op jit(solution)/shard_map/ppermute | solution.py:15
  13.6 3.0 collective-permute-start.7
  16.6 5.7 %collective-permute-start.8 = (bf16[128,512]{0,1:T(8,128)(2,1)S(1)}, bf16[128,512]{0,1:T(8,128)(2,1)}, u32[]{:S(2)}, u32[]{:S(2)}) collective-permute-start(bf16[128,512]{0,1:T(8,128)(2,1)S(1)} %fusion.24), channel_id=1, source_target_pairs={{0,32},{16,48},{32,64},{48,80},{64,96},{80,112},{96,128},{112,144}... | collective-permute-start | bytes 393224 | tf_op jit(solution)/shard_map/ppermute | solution.py:15
  22.3 2.7 collective-permute-start.2
  37.0 3.7 collective-permute-start.3
  41.1 2.8 collective-permute-start.4
  43.9 3.4 collective-permute-done.3
  47.3 2.5 collective-permute-start.5
  49.9 3.1 collective-permute-done.4
  52.9 3.0 collective-permute-start.9
  57.3 2.9 collective-permute-done.1
  61.2 20.7 %all_gather.9 = bf16[128,1024]{1,0:T(8,128)(2,1)S(1)} all-gather(bf16[8,1024]{1,0:T(8,128)(2,1)S(1)} %pad_maximum_fusion.2), channel_id=1, replica_groups=mesh['ctx'=16,'exp'=16] {'ctx'}, dimensions={0}, use_global_device_ids=true | all-gather | bytes 278528 | tf_op jit(solution)/shard_map/all_gather | solution.py:75
  91.4 7.5 %fusion.53 = f32[128,7168]{1,0:T(8,128)} fusion(bf16[128,512]{0,1:T(8,128)(2,1)S(1)} %bitcast.126, bf16[512,7168]{0,1:T(8,128)(2,1)} %all-gather.3.cloned.1.call-done), kind=kOutput, calls=%fused_computation.103 | convolution fusion | flops 939524096 | bytes 11141120 | tf_op jit(solution)/shard_map/dot_general | solution.py:141
  101.5 107.0 %all-reduce.3.cloned.1.call-done = f32[128,7168]{1,0:T(8,128)} async-done(((f32[128,7168]{1,0:T(8,128)}), f32[128,7168]{1,0:T(8,128)}) %all-reduce.3.cloned.1.call-update) | async-done | bytes 3670032
  211.1 15.1 %all_to_all.10 = bf16[16,2,7168]{2,1,0:T(2,128)(2,1)} all-to-all(bf16[16,2,7168]{2,1,0:T(2,128)(2,1)S(1)} %reshape.231), channel_id=1, replica_groups=mesh['ctx'=16,'exp'=16] {'exp'}, dimensions={0} | all-to-all | bytes 917504 | tf_op jit(solution)/shard_map/all_to_all | solution.py:168
  226.5 49.7 %all-gather.5.cloned.1.call-done = bf16[256,2,7168]{2,1,0:T(2,128)(2,1)} async-done(((bf16[16,2,7168]{2,1,0:T(2,128)(2,1)}), bf16[256,2,7168]{2,1,0:T(2,128)(2,1)}) %all-gather.5.cloned.1.call-update) | async-done | bytes 7340048 | tf_op jit(solution)/shard_map/all_gather | solution.py:172
  276.1 15.4 %reshape.232 = bf16[512,7168]{1,0:T(8,128)(2,1)} reshape(bf16[256,2,7168]{2,1,0:T(2,128)(2,1)} %all-gather.5.cloned.1.call-done) | data formatting | bytes 14680064 | tf_op jit(solution)/shard_map/reshape | solution.py:173
  291.5 5.8 %fusion.4 = f32[512,128]{1,0:T(8,128)S(1)} fusion(bf16[512,7168]{1,0:T(8,128)(2,1)} %reshape.232, bf16[1,7168,128]{2,1,0:T(8,128)(2,1)} %param.23), kind=kOutput, calls=%fused_computation.7 | convolution fusion | flops 939524096 | bytes 9437184 | tf_op jit(solution)/shard_map/dot_general | solution.py:174
  297.7 2.1 fusion.19
  299.8 5.0 %convolution_convert_fusion = bf16[256,2,7168]{2,0,1:T(8,128)(2,1)} fusion(bf16[1,128,7168]{2,1,0:T(8,128)(2,1)S(1)} %copy-done, bf16[256,2,128]{2,1,0:T(2,128)(2,1)S(1)} %bitcast.127), kind=kOutput, calls=%fused_computation | convolution fusion | flops 943194112 | bytes 9306112 | tf_op jit(solution)/shard_map/dot_general | solution.py:177
  304.8 67.8 %reduce-scatter.2.cloned.1.call-done = bf16[16,2,7168]{2,0,1:T(8,128)(2,1)} async-done(((bf16[256,2,7168]{2,0,1:T(8,128)(2,1)}), bf16[16,2,7168]{2,0,1:T(8,128)(2,1)}) %reduce-scatter.2.cloned.1.call-update) | async-done | bytes 458768 | tf_op jit(solution)/shard_map/reduce_scatter | solution.py:180
  372.7 2.3 copy.99
  374.9 7.3 %all-to-all-start.1 = ((bf16[16,2,7168]{2,1,0:T(2,128)(2,1)}), bf16[16,2,7168]{2,1,0:T(2,128)(2,1)S(1)}, u32[]{:S(2)}, u32[]{:S(2)}) async-start(bf16[16,2,7168]{2,1,0:T(2,128)(2,1)} %copy.99), calls=%async_computation.2 | async-start | bytes 917504 | tf_op jit(solution)/shard_map/all_to_all | solution.py:183
  382.3 8.3 %all-to-all-done.1 = bf16[16,2,7168]{2,1,0:T(2,128)(2,1)S(1)} async-done(((bf16[16,2,7168]{2,1,0:T(2,128)(2,1)}), bf16[16,2,7168]{2,1,0:T(2,128)(2,1)S(1)}, u32[]{:S(2)}, u32[]{:S(2)}) %all-to-all-start.1) | async-done | bytes 458784 | tf_op jit(solution)/shard_map/all_to_all | solution.py:183
  (118 shorter events, 33.1 us)
Async XLA Ops:
  6.5 293.3 %copy-start = (bf16[1,128,7168]{2,1,0:T(8,128)(2,1)S(1)}, bf16[1,128,7168]{2,1,0:T(8,128)(2,1)}, u32[]{:S(2)}) copy-start(bf16[1,128,7168]{2,1,0:T(8,128)(2,1)} %param.25) | copy-start | bytes 5505028
  6.5 34.1 %copy-start.2 = (bf16[128,512]{1,0:T(8,128)(2,1)S(1)}, bf16[128,512]{1,0:T(8,128)(2,1)}, u32[]{:S(2)}) copy-start(bf16[128,512]{1,0:T(8,128)(2,1)} %param.14) | copy-start | bytes 393220
  6.5 30.4 %copy-start.4 = (bf16[128,512]{1,0:T(8,128)(2,1)S(1)}, bf16[128,512]{1,0:T(8,128)(2,1)}, u32[]{:S(2)}) copy-start(bf16[128,512]{1,0:T(8,128)(2,1)} %param.15) | copy-start | bytes 393220
  6.5 29.2 %copy-start.5 = (bf16[128,512]{1,0:T(8,128)(2,1)S(1)}, bf16[128,512]{1,0:T(8,128)(2,1)}, u32[]{:S(2)}) copy-start(bf16[128,512]{1,0:T(8,128)(2,1)} %param.13) | copy-start | bytes 393220
  6.5 84.8 %all-gather.3.cloned.1.call-start = ((), (), s32[]{:S(2)}) async-start(), calls=%async_computation.3 | async-start | bytes 7798784 | tf_op jit(solution)/shard_map/all_gather | solution.py:143
  7.3 201.3 %all-reduce.3.cloned.1.call-start = ((), (), s32[]{:S(2)}) async-start(), calls=%async_computation.6 | async-start | bytes 7340032
  8.4 73.4 %collective-permute-start.6 = (bf16[128,512]{0,1:T(8,128)(2,1)S(1)}, bf16[128,512]{0,1:T(8,128)(2,1)S(1)}, u32[]{:S(2)}, u32[]{:S(2)}) collective-permute-start(bf16[128,512]{0,1:T(8,128)(2,1)S(1)} %fusion.24), channel_id=1, source_target_pairs={{0,64},{16,80},{32,96},{48,112},{64,128},{80,144},{96,160},{112,17... | collective-permute-start | bytes 393224 | tf_op jit(solution)/shard_map/ppermute | solution.py:15
  13.6 68.3 %collective-permute-start.7 = (bf16[128,512]{0,1:T(8,128)(2,1)S(1)}, bf16[128,512]{0,1:T(8,128)(2,1)S(1)}, u32[]{:S(2)}, u32[]{:S(2)}) collective-permute-start(bf16[128,512]{0,1:T(8,128)(2,1)S(1)} %fusion.24), channel_id=1, source_target_pairs={{0,48},{16,64},{32,80},{48,96},{64,112},{80,128},{96,144},{112,160... | collective-permute-start | bytes 393224 | tf_op jit(solution)/shard_map/ppermute | solution.py:15
  16.6 66.7 %collective-permute-start.8 = (bf16[128,512]{0,1:T(8,128)(2,1)S(1)}, bf16[128,512]{0,1:T(8,128)(2,1)}, u32[]{:S(2)}, u32[]{:S(2)}) collective-permute-start(bf16[128,512]{0,1:T(8,128)(2,1)S(1)} %fusion.24), channel_id=1, source_target_pairs={{0,32},{16,48},{32,64},{48,80},{64,96},{80,112},{96,128},{112,144}... | collective-permute-start | bytes 393224 | tf_op jit(solution)/shard_map/ppermute | solution.py:15
  22.3 18.8 %collective-permute-start.2 = (bf16[128,512]{1,0:T(8,128)(2,1)}, bf16[128,512]{1,0:T(8,128)(2,1)S(1)}, u32[]{:S(2)}, u32[]{:S(2)}) collective-permute-start(bf16[128,512]{1,0:T(8,128)(2,1)} %param.15), channel_id=1, source_target_pairs={{0,64},{16,80},{32,96},{48,112},{64,128},{80,144},{96,160},{112,17... | collective-permute-start | bytes 393224 | tf_op jit(solution)/shard_map/ppermute | solution.py:15
  26.4 10.6 %collective-permute-start = (bf16[16,512]{1,0:T(8,128)(2,1)}, bf16[16,512]{1,0:T(8,128)(2,1)S(1)}, u32[]{:S(2)}, u32[]{:S(2)}) collective-permute-start(bf16[16,512]{1,0:T(8,128)(2,1)} %slice.66), channel_id=1, source_target_pairs={{16,0},{32,16},{48,32},{64,48},{80,64},{96,80},{112,96},{128,112},... | collective-permute-start | bytes 49160 | tf_op jit(solution)/shard_map/ppermute | solution.py:15
  37.0 10.3 %collective-permute-start.3 = (bf16[128,512]{1,0:T(8,128)(2,1)S(1)}, bf16[128,512]{1,0:T(8,128)(2,1)S(1)}, u32[]{:S(2)}, u32[]{:S(2)}) collective-permute-start(bf16[128,512]{1,0:T(8,128)(2,1)S(1)} %copy-done.4), channel_id=1, source_target_pairs={{0,48},{16,64},{32,80},{48,96},{64,112},{80,128},{96,144},{112,160... | collective-permute-start | bytes 393224 | tf_op jit(solution)/shard_map/ppermute | solution.py:15
  41.1 11.8 %collective-permute-start.4 = (bf16[128,512]{1,0:T(8,128)(2,1)S(1)}, bf16[128,512]{1,0:T(8,128)(2,1)S(1)}, u32[]{:S(2)}, u32[]{:S(2)}) collective-permute-start(bf16[128,512]{1,0:T(8,128)(2,1)S(1)} %copy-done.4), channel_id=1, source_target_pairs={{0,32},{16,48},{32,64},{48,80},{64,96},{80,112},{96,128},{112,144}... | collective-permute-start | bytes 393224 | tf_op jit(solution)/shard_map/ppermute | solution.py:15
  47.3 8.7 %collective-permute-start.5 = (bf16[128,512]{1,0:T(8,128)(2,1)S(1)}, bf16[128,512]{1,0:T(8,128)(2,1)S(1)}, u32[]{:S(2)}, u32[]{:S(2)}) collective-permute-start(bf16[128,512]{1,0:T(8,128)(2,1)S(1)} %copy-done.4), channel_id=1, source_target_pairs={{0,16},{16,32},{32,48},{48,64},{64,80},{80,96},{96,112},{112,128},... | collective-permute-start | bytes 393224 | tf_op jit(solution)/shard_map/ppermute | solution.py:15
  52.9 32.0 %collective-permute-start.9 = (bf16[128,512]{0,1:T(8,128)(2,1)S(1)}, bf16[128,512]{0,1:T(8,128)(2,1)}, u32[]{:S(2)}, u32[]{:S(2)}) collective-permute-start(bf16[128,512]{0,1:T(8,128)(2,1)S(1)} %fusion.24), channel_id=1, source_target_pairs={{0,16},{16,32},{32,48},{48,64},{64,80},{80,96},{96,112},{112,128},... | collective-permute-start | bytes 393224 | tf_op jit(solution)/shard_map/ppermute | solution.py:15
  56.0 4.2 %collective-permute-start.1 = (bf16[16,512]{1,0:T(8,128)(2,1)S(1)}, bf16[16,512]{1,0:T(8,128)(2,1)S(1)}, u32[]{:S(2)}, u32[]{:S(2)}) collective-permute-start(bf16[16,512]{1,0:T(8,128)(2,1)S(1)} %slice.74), channel_id=1, source_target_pairs={{16,0},{32,16},{48,32},{64,48},{80,64},{96,80},{112,96},{128,112},... | collective-permute-start | bytes 49160 | tf_op jit(solution)/shard_map/ppermute | solution.py:15
  60.2 30.5 %copy-start.9 = (f32[128,4]{0,1:T(4,128)S(1)}, f32[128,4]{0,1:T(4,128)}, u32[]{:S(2)}) copy-start(f32[128,4]{0,1:T(4,128)} %get-tuple-element.10) | copy-start | bytes 6148
  82.8 8.4 %copy-start.8 = (f32[128,4]{0,1:T(4,128)S(1)}, f32[128,4]{0,1:T(4,128)}, u32[]{:S(2)}) copy-start(f32[128,4]{0,1:T(4,128)} %get-tuple-element.9) | copy-start | bytes 6148
  98.9 109.6 %copy-start.3 = (bf16[8,7168]{1,0:T(8,128)(2,1)S(1)}, bf16[8,7168]{1,0:T(8,128)(2,1)}, u32[]{:S(2)}) copy-start(bf16[8,7168]{1,0:T(8,128)(2,1)} %param.19) | copy-start | bytes 344068
  98.9 110.8 %copy-start.6 = (f32[7168]{0:T(1024)S(1)}, f32[7168]{0:T(1024)}, u32[]{:S(2)}) copy-start(f32[7168]{0:T(1024)} %param.20) | copy-start | bytes 86020
  98.9 177.2 %all-gather.5.cloned.1.call-start = ((), (), s32[]{:S(2)}) async-start(), calls=%async_computation.4 | async-start | bytes 7798784 | tf_op jit(solution)/shard_map/all_gather | solution.py:172
  226.2 146.4 %reduce-scatter.2.cloned.1.call-start = ((), (), s32[]{:S(2)}) async-start(), calls=%async_computation.5 | async-start | bytes 7798784 | tf_op jit(solution)/shard_map/reduce_scatter | solution.py:180
  304.8 77.4 %copy-start.11 = (f32[8,2]{0,1:T(2,128)S(1)}, f32[8,2]{0,1:T(2,128)}, u32[]{:S(2)}) copy-start(f32[8,2]{0,1:T(2,128)} %param.22) | copy-start | bytes 196
  374.9 15.6 %all-to-all-start.1 = ((bf16[16,2,7168]{2,1,0:T(2,128)(2,1)}), bf16[16,2,7168]{2,1,0:T(2,128)(2,1)S(1)}, u32[]{:S(2)}, u32[]{:S(2)}) async-start(bf16[16,2,7168]{2,1,0:T(2,128)(2,1)} %copy.99), calls=%async_computation.2 | async-start | bytes 917504 | tf_op jit(solution)/shard_map/all_to_all | solution.py:183
  (5 other events, 14.8 us)
Sparse Core Ops, SparseCore 0:
  9.2 71.2 all-gather.2
  99.1 109.4 all-reduce.2
  226.3 49.7 all-gather.4
  305.0 67.6 reduce-scatter.1
